TPU v7x, 32 devices: a whole 2x2x4 slice. The times are simulated.
32 devices in a mesh: tens: 2 (over y), atom: 16 (over z, x, core).
Axes of the slice: x: 2, y: 2, z: 4, core: 2. Of those that a mesh axis runs over, the one named last changes fastest.
Arguments:
- chibar: float32 [96, 4096], P(None, 'atom'), may hold values from -6 to 6
- t_blocks: float32 [384, 196608], P(None, ('tens', 'atom')), may hold values from -0.3125 to 0.3125
- n_saved: float32 [96, 196608], P('tens', 'atom'), may hold values from -0.078125 to 0.078125
- q_list: int32 [2, 16, 3], P('tens', 'atom'), may hold values from 0 to 13, as said below
- q_count: int32 [2, 16], P('tens', 'atom'), may hold values from 1 to 3, as said below
Outputs:
- gbar: float32 [1024, 320], P('atom')
Inputs may be any that keep to these rules, and one draw needn't show every extreme that they name: `q_list`: the 3 entries of one pair owner's list name blocks of 3 distinct atom indices. `q_count`: equal to 3 on at least one pair owner.
All inputs are finite; a program needn't handle non-finite values.
Results may differ from a plain program's by a relative error of at most 0.0003.
Values sent between devices are 32-bit elements; how exact they have to be, the bound alone decides.
No kernel may reach another device: no remote copies, remote signals or barrier semaphores. Data moves between devices by JAX's collectives and lax.ppermute only.
A program may use at most 64 MiB of HBM per device.

v0:
```python
import jax
import jax.numpy as jnp
from jax import lax
from jax.sharding import PartitionSpec as P

BLK = 128
ORB_DEV = 64
QB_DEV = 2
REACH = 3
QL = 3


def shifted(x, axis, by):
    devices = lax.axis_size(axis)
    return lax.ppermute(x, axis, [(i, (i + by) % devices) for i in range(devices)])


def place_block(block, offset, orb_width):
    return jnp.pad(block, ((0, 0), (offset * orb_width, (2 - offset) * orb_width)))


def assemble(blocks):
    moved = []
    for by_step, row_block in ((1, 2), (-1, 0)):
        moved.append(shifted(blocks[row_block], "atom", by_step))
    return (
        place_block(moved[0], 0, ORB_DEV)
        + place_block(blocks[1], 1, ORB_DEV)
        + place_block(moved[1], 2, ORB_DEV)
    )


def local(chibar, t_blocks, n_saved, q_list, q_count):
    highest = lax.Precision.HIGHEST
    p_window = chibar.shape[0]
    band_width = 3 * ORB_DEV
    slot_ids = q_list.reshape(QL)
    in_use = q_count.reshape(())
    keeper = (jnp.arange(QL) < in_use).astype(jnp.float32)
    pieces = []
    for offset in range(-REACH, REACH + 1):
        if offset == 0:
            pieces.append(chibar)
        else:
            pieces.append(shifted(chibar, "atom", -offset))
    neighbour = jnp.concatenate(pieces, axis=1).reshape(p_window, (2 * REACH + 1) * QB_DEV, BLK)
    chosen = jnp.take(neighbour, slot_ids, axis=1)
    chosen = (chosen * keeper[None, :, None]).reshape(p_window, QL * BLK)
    mbar_local = jnp.dot(chosen, t_blocks, precision=highest, preferred_element_type=jnp.float32)
    regrouped = lax.all_to_all(mbar_local, "tens", split_axis=0, concat_axis=1, tiled=True)
    p_rows = regrouped.shape[0]
    partial_value = jnp.einsum(
        "pnm,pml->nl",
        regrouped.reshape(p_rows, band_width, ORB_DEV),
        n_saved.reshape(p_rows, ORB_DEV, band_width),
        precision=highest,
    )
    result = lax.psum(assemble(partial_value.reshape(3, ORB_DEV, band_width)), "tens")
    return result


def solution(mesh):
    placed = (
        P(None, "atom"),
        P(None, ("tens", "atom")),
        P("tens", "atom"),
        P("tens", "atom", None),
        P("tens", "atom"),
    )
    return jax.shard_map(
        local, mesh=mesh, in_specs=placed, out_specs=P("atom", None), check_vma=False
    )
```

profile of v0, /device:TPU:0, one launch (start us, length us, event | category | flops | bytes accessed | tf_op | source)
XLA Modules:
  0.0 120.9 jit_solution(3969552200305108274)
XLA Ops:
  6.5 6.0 %collective-permute-start.4 = (f32[96,256]{1,0:T(8,128)}, f32[96,256]{1,0:T(8,128)S(1)}, u32[]{:S(2)}, u32[]{:S(2)}) collective-permute-start(f32[96,256]{1,0:T(8,128)} %param.5), channel_id=1, source_target_pairs={{0,14},{1,15},{2,0},{3,1},{4,2},{5,3},{6,4},{7,5},{8,6},{9,7},{10,... | collective-permute-start | bytes 294920 | tf_op jit(solution)/shard_map/ppermute | solution.py:15
  12.5 0.5 collective-permute-start.2
  13.1 0.7 collective-permute-start.1
  13.7 0.7 fusion.7
  14.4 0.7 compare_and_fusion
  15.9 3.9 %collective-permute-done = f32[96,256]{1,0:T(8,128)S(1)} collective-permute-done((f32[96,256]{1,0:T(8,128)}, f32[96,256]{1,0:T(8,128)S(1)}, u32[]{:S(2)}, u32[]{:S(2)}) %collective-permute-start) | collective-permute-done | bytes 98336 | tf_op jit(solution)/shard_map/ppermute | solution.py:15
  19.8 2.7 %collective-permute-start.5 = (f32[96,256]{1,0:T(8,128)}, f32[96,256]{1,0:T(8,128)S(1)}, u32[]{:S(2)}, u32[]{:S(2)}) collective-permute-start(f32[96,256]{1,0:T(8,128)} %param.5), channel_id=1, source_target_pairs={{0,13},{1,14},{2,15},{3,0},{4,1},{5,2},{6,3},{7,4},{8,5},{9,6},{10... | collective-permute-start | bytes 294920 | tf_op jit(solution)/shard_map/ppermute | solution.py:15
  22.6 0.9 constant_dynamic-update-slice_fusion.3
  23.5 2.0 %collective-permute-done.5 = f32[96,256]{1,0:T(8,128)S(1)} collective-permute-done((f32[96,256]{1,0:T(8,128)}, f32[96,256]{1,0:T(8,128)S(1)}, u32[]{:S(2)}, u32[]{:S(2)}) %collective-permute-start.5) | collective-permute-done | bytes 98336 | tf_op jit(solution)/shard_map/ppermute | solution.py:15
  25.6 0.6 gather_fusion
  26.2 0.1 copy.7
  26.4 9.1 %fusion = f32[2,48,6144]{2,1,0:T(8,128)} fusion(f32[384,6144]{1,0:T(8,128)} %param.6, f32[2,48,384]{2,1,0:T(8,128)S(1)} %gather.7, f32[384]{0:T(512)S(1)} %broadcast_bitcast_fusion, pred[384]{0:T(512)(128)(4,1)S(1)} %broadcast_bitcast_fusion.1), kind=kOutput, calls=%fused_computation.1 | convolution fusion | flops 2717982720 | bytes 11945856 | tf_op jit(solution)/shard_map/dot_general | solution.py:49
  35.5 4.9 %all-to-all-start = ((f32[2,48,6144]{2,1,0:T(8,128)}), f32[2,48,6144]{2,1,0:T(8,128)}, u32[]{:S(2)}, u32[]{:S(2)}) async-start(f32[2,48,6144]{2,1,0:T(8,128)} %fusion), calls=%async_computation | async-start | bytes 4718592 | tf_op jit(solution)/shard_map/all_to_all | solution.py:50
  40.5 2.7 %reshape.88 = f32[48,64,192]{2,1,0:T(8,128)S(1)} reshape(f32[48,12288]{1,0:T(8,128)} %param.7) | data formatting | bytes 4718592 | tf_op jit(solution)/shard_map/reshape | solution.py:55
  43.2 24.1 %all-to-all-done = f32[2,48,6144]{2,1,0:T(8,128)} async-done(((f32[2,48,6144]{2,1,0:T(8,128)}), f32[2,48,6144]{2,1,0:T(8,128)}, u32[]{:S(2)}, u32[]{:S(2)}) %all-to-all-start) | async-done | bytes 2359328 | tf_op jit(solution)/shard_map/all_to_all | solution.py:50
  67.3 4.9 %copy.8 = f32[48,2,6144]{2,1,0:T(2,128)} copy(f32[48,2,6144]{2,0,1:T(8,128)} %bitcast.8) | data formatting | bytes 4718592 | tf_op jit(solution)/shard_map/all_to_all | solution.py:50
  72.2 5.5 %reshape.87 = f32[48,192,64]{2,1,0:T(8,128)} reshape(f32[48,2,6144]{2,1,0:T(2,128)} %copy.8) | data formatting | bytes 4718592 | tf_op jit(solution)/shard_map/reshape | solution.py:54
  77.8 5.9 %convolution_bitcast_fusion = f32[192,192]{1,0:T(8,128)S(1)} fusion(f32[48,192,64]{2,1,0:T(8,128)} %reshape.87, f32[48,64,192]{2,1,0:T(8,128)S(1)} %reshape.88), kind=kOutput, calls=%fused_computation.3 | convolution fusion | flops 1358954496 | bytes 4866048 | tf_op jit(solution)/shard_map/pnm,pml->nl/dot_general | solution.py:52
  83.7 2.1 %collective-permute-start.6 = (f32[64,192]{1,0:T(8,128)S(1)}, f32[64,192]{1,0:T(8,128)S(1)}, u32[]{:S(2)}, u32[]{:S(2)}) collective-permute-start(f32[64,192]{1,0:T(8,128)S(1)} %get-tuple-element.5), channel_id=1, source_target_pairs={{0,1},{1,2},{2,3},{3,4},{4,5},{5,6},{6,7},{7,8},{8,9},{9,10},{10,1... | collective-permute-start | bytes 147464 | tf_op jit(solution)/shard_map/ppermute | solution.py:15
  85.9 2.4 %collective-permute-start.7 = (f32[64,192]{1,0:T(8,128)S(1)}, f32[64,192]{1,0:T(8,128)S(1)}, u32[]{:S(2)}, u32[]{:S(2)}) collective-permute-start(f32[64,192]{1,0:T(8,128)S(1)} %get-tuple-element.6), channel_id=1, source_target_pairs={{0,15},{1,0},{2,1},{3,2},{4,3},{5,4},{6,5},{7,6},{8,7},{9,8},{10,9... | collective-permute-start | bytes 147464 | tf_op jit(solution)/shard_map/ppermute | solution.py:15
  88.2 2.0 %collective-permute-done.6 = f32[64,192]{1,0:T(8,128)S(1)} collective-permute-done((f32[64,192]{1,0:T(8,128)S(1)}, f32[64,192]{1,0:T(8,128)S(1)}, u32[]{:S(2)}, u32[]{:S(2)}) %collective-permute-start.6) | collective-permute-done | bytes 49184 | tf_op jit(solution)/shard_map/ppermute | solution.py:15
  90.3 0.7 pad_add_fusion
  91.0 21.5 %all-reduce.5.cloned.1.call-done = f32[64,320]{1,0:T(8,128)} async-done(((f32[64,320]{1,0:T(8,128)}), f32[64,320]{1,0:T(8,128)}) %all-reduce.5.cloned.1.call-update) | async-done | bytes 81936 | tf_op jit(solution)/shard_map/psum | solution.py:58
  112.5 1.5 %copy.21 = f32[64,320]{1,0:T(8,128)} copy(f32[64,320]{1,0:T(8,128)} %all-reduce.5.cloned.1.call-done) | data formatting | bytes 163840
  (22 shorter events, 0.4 us)
Async XLA Ops:
  6.5 17.0 %collective-permute-start.4 = (f32[96,256]{1,0:T(8,128)}, f32[96,256]{1,0:T(8,128)S(1)}, u32[]{:S(2)}, u32[]{:S(2)}) collective-permute-start(f32[96,256]{1,0:T(8,128)} %param.5), channel_id=1, source_target_pairs={{0,14},{1,15},{2,0},{3,1},{4,2},{5,3},{6,4},{7,5},{8,6},{9,7},{10,... | collective-permute-start | bytes 294920 | tf_op jit(solution)/shard_map/ppermute | solution.py:15
  12.5 10.9 %collective-permute-start.3 = (f32[96,256]{1,0:T(8,128)}, f32[96,256]{1,0:T(8,128)S(1)}, u32[]{:S(2)}, u32[]{:S(2)}) collective-permute-start(f32[96,256]{1,0:T(8,128)} %param.5), channel_id=1, source_target_pairs={{0,15},{1,0},{2,1},{3,2},{4,3},{5,4},{6,5},{7,6},{8,7},{9,8},{10,9... | collective-permute-start | bytes 294920 | tf_op jit(solution)/shard_map/ppermute | solution.py:15
  12.5 10.0 %collective-permute-start.2 = (f32[96,256]{1,0:T(8,128)}, f32[96,256]{1,0:T(8,128)S(1)}, u32[]{:S(2)}, u32[]{:S(2)}) collective-permute-start(f32[96,256]{1,0:T(8,128)} %param.5), channel_id=1, source_target_pairs={{0,1},{1,2},{2,3},{3,4},{4,5},{5,6},{6,7},{7,8},{8,9},{9,10},{10,1... | collective-permute-start | bytes 294920 | tf_op jit(solution)/shard_map/ppermute | solution.py:15
  13.1 9.5 %collective-permute-start.1 = (f32[96,256]{1,0:T(8,128)}, f32[96,256]{1,0:T(8,128)S(1)}, u32[]{:S(2)}, u32[]{:S(2)}) collective-permute-start(f32[96,256]{1,0:T(8,128)} %param.5), channel_id=1, source_target_pairs={{0,2},{1,3},{2,4},{3,5},{4,6},{5,7},{6,8},{7,9},{8,10},{9,11},{10,... | collective-permute-start | bytes 294920 | tf_op jit(solution)/shard_map/ppermute | solution.py:15
  13.7 6.1 %collective-permute-start = (f32[96,256]{1,0:T(8,128)}, f32[96,256]{1,0:T(8,128)S(1)}, u32[]{:S(2)}, u32[]{:S(2)}) collective-permute-start(f32[96,256]{1,0:T(8,128)} %param.5), channel_id=1, source_target_pairs={{0,3},{1,4},{2,5},{3,6},{4,7},{5,8},{6,9},{7,10},{8,11},{9,12},{10... | collective-permute-start | bytes 294920 | tf_op jit(solution)/shard_map/ppermute | solution.py:15
  19.8 5.8 %collective-permute-start.5 = (f32[96,256]{1,0:T(8,128)}, f32[96,256]{1,0:T(8,128)S(1)}, u32[]{:S(2)}, u32[]{:S(2)}) collective-permute-start(f32[96,256]{1,0:T(8,128)} %param.5), channel_id=1, source_target_pairs={{0,13},{1,14},{2,15},{3,0},{4,1},{5,2},{6,3},{7,4},{8,5},{9,6},{10... | collective-permute-start | bytes 294920 | tf_op jit(solution)/shard_map/ppermute | solution.py:15
  35.5 31.8 %all-to-all-start = ((f32[2,48,6144]{2,1,0:T(8,128)}), f32[2,48,6144]{2,1,0:T(8,128)}, u32[]{:S(2)}, u32[]{:S(2)}) async-start(f32[2,48,6144]{2,1,0:T(8,128)} %fusion), calls=%async_computation | async-start | bytes 4718592 | tf_op jit(solution)/shard_map/all_to_all | solution.py:50
  40.4 72.1 %all-reduce.5.cloned.1.call-start = ((), (), s32[]{:S(2)}) async-start(), calls=%async_computation.1 | async-start | bytes 196608 | tf_op jit(solution)/shard_map/psum | solution.py:58
  83.7 6.5 %collective-permute-start.6 = (f32[64,192]{1,0:T(8,128)S(1)}, f32[64,192]{1,0:T(8,128)S(1)}, u32[]{:S(2)}, u32[]{:S(2)}) collective-permute-start(f32[64,192]{1,0:T(8,128)S(1)} %get-tuple-element.5), channel_id=1, source_target_pairs={{0,1},{1,2},{2,3},{3,4},{4,5},{5,6},{6,7},{7,8},{8,9},{9,10},{10,1... | collective-permute-start | bytes 147464 | tf_op jit(solution)/shard_map/ppermute | solution.py:15
  85.9 4.4 %collective-permute-start.7 = (f32[64,192]{1,0:T(8,128)S(1)}, f32[64,192]{1,0:T(8,128)S(1)}, u32[]{:S(2)}, u32[]{:S(2)}) collective-permute-start(f32[64,192]{1,0:T(8,128)S(1)} %get-tuple-element.6), channel_id=1, source_target_pairs={{0,15},{1,0},{2,1},{3,2},{4,3},{5,4},{6,5},{7,6},{8,7},{9,8},{10,9... | collective-permute-start | bytes 147464 | tf_op jit(solution)/shard_map/ppermute | solution.py:15
Sparse Core Ops, SparseCore 0:
  91.2 21.3 all-reduce.4
where the time goes:
time: 121 us
  waiting for transfers between devices  53.6 us (44%)
  starting transfers between devices  19.3 us (16%)
  local copies, waits for them, and re-layouts  16.6 us (14%)
  matrix products  15 us (12%)
  between operations  14.2 us (12%)
  other arithmetic  2.07 us (2%)
    all_to_all x1, waiting for transfers between devices, local(): lax.all_to_all(mbar_local, 'tens', split_axis=0, concat_axis=1, tiled=True)  24.1 us
    psum x1, waiting for transfers between devices, local(): lax.psum(assemble(partial_value.reshape(3, ORB_DEV, band_width)), 'tens')  21.5 us
    ppermute x8, starting transfers between devices, shifted(): lax.ppermute(x, axis, [(i, (i + by) % devices) for i in range(devices)])  14.4 us
    dot_general x1, matrix products, local(): jnp.dot(chosen, t_blocks, precision=highest, preferred_element_type=jnp.f...  9.12 us
    ppermute x8, waiting for transfers between devices, shifted(): lax.ppermute(x, axis, [(i, (i + by) % devices) for i in range(devices)])  8.05 us
    dot_general x1, matrix products, local(): jnp.einsum('pnm,pml->nl', regrouped.reshape(p_rows, band_width, ORB_DEV),...  5.92 us
    reshape x1, local copies, waits for them, and re-layouts, local(): regrouped.reshape(p_rows, band_width, ORB_DEV)  5.54 us
    all_to_all x1, local copies, waits for them, and re-layouts, local(): lax.all_to_all(mbar_local, 'tens', split_axis=0, concat_axis=1, tiled=True)  4.91 us
  transfers between devices with their start and end apart: 10, of which 5 were waited for; matrix products, arithmetic and copies ran while one was open for 4% of the time, Pallas kernels for 0%

commit v1 on v0

--- a/solution.py
+++ b/solution.py
@@ -8,6 +8,7 @@
 QB_DEV = 2
 REACH = 3
 QL = 3
+map_joints_all = lambda t0, net_axis: jnp.sum(lax.all_gather(t0, net_axis), 0)
 
 
 def shifted(x, axis, by):
@@ -55,7 +56,7 @@
         n_saved.reshape(p_rows, ORB_DEV, band_width),
         precision=highest,
     )
-    result = lax.psum(assemble(partial_value.reshape(3, ORB_DEV, band_width)), "tens")
+    result = map_joints_all(assemble(partial_value.reshape(3, ORB_DEV, band_width)), "tens")
     return result
 
 

time: 121 us -> 90.4 us (0.75)
  waiting for transfers between devices: 53.6 us -> 32.2 us
  between operations: 14.2 us -> 0.8 us
  blocking collectives: 0 us -> 5.41 us
  local copies, waits for them, and re-layouts: 16.6 us -> 15.1 us
    psum x1 -> x0, waiting for transfers between devices: 21.5 us -> none  [local(): lax.psum(assemble(partial_value.reshape(3, ORB_DEV, band_width)), 'tens')]
    all_gather x0 -> x1, blocking collectives: none -> 5.41 us  [lax.all_gather(t0, net_axis)]
    unnamed x7 -> x6, local copies, waits for them, and re-layouts: 2.5 us -> 0.96 us
  transfers between devices with their start and end apart: 10 -> 9, of which waited for: 5 -> 4; matrix products, arithmetic and copies ran while one was open for 4% -> 6% of each run, Pallas kernels for 0% -> 0%
where the time goes in v1:
time: 90.4 us; the launch traced here: 90 us
  waiting for transfers between devices  32.2 us (36%)
  starting transfers between devices  19.3 us (21%)
  local copies, waits for them, and re-layouts  15.1 us (17%)
  matrix products  15.1 us (17%)
  blocking collectives  5.41 us (6%)
  other arithmetic  2.07 us (2%)
    all_to_all x1, waiting for transfers between devices, local(): lax.all_to_all(mbar_local, 'tens', split_axis=0, concat_axis=1, tiled=True)  24.2 us
    ppermute x8, starting transfers between devices, shifted(): lax.ppermute(x, axis, [(i, (i + by) % devices) for i in range(devices)])  14.4 us
    dot_general x1, matrix products, local(): jnp.dot(chosen, t_blocks, precision=highest, preferred_element_type=jnp.f...  9.19 us
    ppermute x8, waiting for transfers between devices, shifted(): lax.ppermute(x, axis, [(i, (i + by) % devices) for i in range(devices)])  8.05 us
    dot_general x1, matrix products, local(): jnp.einsum('pnm,pml->nl', regrouped.reshape(p_rows, band_width, ORB_DEV),...  5.92 us
    reshape x1, local copies, waits for them, and re-layouts, local(): regrouped.reshape(p_rows, band_width, ORB_DEV)  5.55 us
    all_gather x1, blocking collectives, lax.all_gather(t0, net_axis)  5.41 us
    all_to_all x1, local copies, waits for them, and re-layouts, local(): lax.all_to_all(mbar_local, 'tens', split_axis=0, concat_axis=1, tiled=True)  4.92 us
  transfers between devices with their start and end apart: 9, of which 4 were waited for; matrix products, arithmetic and copies ran while one was open for 6% of the time, Pallas kernels for 0%

profile of v1, /device:TPU:0, one launch (start us, length us, event | category | flops | bytes accessed | tf_op | source)
XLA Modules:
  0.0 90.0 jit_solution(13542987127607456014)
XLA Ops:
  0.0 6.0 %collective-permute-start.4 = (f32[96,256]{1,0:T(8,128)}, f32[96,256]{1,0:T(8,128)S(1)}, u32[]{:S(2)}, u32[]{:S(2)}) collective-permute-start(f32[96,256]{1,0:T(8,128)} %param.5), channel_id=1, source_target_pairs={{0,14},{1,15},{2,0},{3,1},{4,2},{5,3},{6,4},{7,5},{8,6},{9,7},{10,... | collective-permute-start | bytes 294920 | tf_op jit(solution)/shard_map/ppermute | solution.py:16
  6.0 0.5 collective-permute-start.2
  6.5 0.7 collective-permute-start.1
  7.2 0.7 fusion.7
  7.9 0.7 compare_and_fusion
  9.3 3.9 %collective-permute-done = f32[96,256]{1,0:T(8,128)S(1)} collective-permute-done((f32[96,256]{1,0:T(8,128)}, f32[96,256]{1,0:T(8,128)S(1)}, u32[]{:S(2)}, u32[]{:S(2)}) %collective-permute-start) | collective-permute-done | bytes 98336 | tf_op jit(solution)/shard_map/ppermute | solution.py:16
  13.3 2.7 %collective-permute-start.5 = (f32[96,256]{1,0:T(8,128)}, f32[96,256]{1,0:T(8,128)S(1)}, u32[]{:S(2)}, u32[]{:S(2)}) collective-permute-start(f32[96,256]{1,0:T(8,128)} %param.5), channel_id=1, source_target_pairs={{0,13},{1,14},{2,15},{3,0},{4,1},{5,2},{6,3},{7,4},{8,5},{9,6},{10... | collective-permute-start | bytes 294920 | tf_op jit(solution)/shard_map/ppermute | solution.py:16
  16.0 0.9 %constant_dynamic-update-slice_fusion.3 = f32[96,1792]{1,0:T(8,128)S(1)} fusion(f32[96,1792]{1,0:T(8,128)S(1)} %constant_dynamic-update-slice_fusion.4, f32[96,256]{1,0:T(8,128)} %param.5), kind=kLoop, calls=%fused_computation.14 | loop fusion | bytes 196608
  17.0 2.0 %collective-permute-done.5 = f32[96,256]{1,0:T(8,128)S(1)} collective-permute-done((f32[96,256]{1,0:T(8,128)}, f32[96,256]{1,0:T(8,128)S(1)}, u32[]{:S(2)}, u32[]{:S(2)}) %collective-permute-start.5) | collective-permute-done | bytes 98336 | tf_op jit(solution)/shard_map/ppermute | solution.py:16
  19.1 0.6 gather_fusion
  19.7 0.1 copy.7
  19.9 9.2 %fusion = f32[2,48,6144]{2,1,0:T(8,128)} fusion(f32[384,6144]{1,0:T(8,128)} %param.6, f32[2,48,384]{2,1,0:T(8,128)S(1)} %gather.7, f32[384]{0:T(512)S(1)} %broadcast_bitcast_fusion, pred[384]{0:T(512)(128)(4,1)S(1)} %broadcast_bitcast_fusion.1), kind=kOutput, calls=%fused_computation.1 | convolution fusion | flops 2717982720 | bytes 11945856 | tf_op jit(solution)/shard_map/dot_general | solution.py:50
  29.1 4.9 %all-to-all-start = ((f32[2,48,6144]{2,1,0:T(8,128)}), f32[2,48,6144]{2,1,0:T(8,128)}, u32[]{:S(2)}, u32[]{:S(2)}) async-start(f32[2,48,6144]{2,1,0:T(8,128)} %fusion), calls=%async_computation | async-start | bytes 4718592 | tf_op jit(solution)/shard_map/all_to_all | solution.py:51
  34.0 2.7 %reshape.88 = f32[48,64,192]{2,1,0:T(8,128)S(1)} reshape(f32[48,12288]{1,0:T(8,128)} %param.7) | data formatting | bytes 4718592 | tf_op jit(solution)/shard_map/reshape | solution.py:56
  36.7 24.2 %all-to-all-done = f32[2,48,6144]{2,1,0:T(8,128)} async-done(((f32[2,48,6144]{2,1,0:T(8,128)}), f32[2,48,6144]{2,1,0:T(8,128)}, u32[]{:S(2)}, u32[]{:S(2)}) %all-to-all-start) | async-done | bytes 2359328 | tf_op jit(solution)/shard_map/all_to_all | solution.py:51
  60.9 4.9 %copy.8 = f32[48,2,6144]{2,1,0:T(2,128)} copy(f32[48,2,6144]{2,0,1:T(8,128)} %bitcast.8) | data formatting | bytes 4718592 | tf_op jit(solution)/shard_map/all_to_all | solution.py:51
  65.8 5.6 %reshape.87 = f32[48,192,64]{2,1,0:T(8,128)} reshape(f32[48,2,6144]{2,1,0:T(2,128)} %copy.8) | data formatting | bytes 4718592 | tf_op jit(solution)/shard_map/reshape | solution.py:55
  71.4 5.9 %convolution_bitcast_fusion = f32[192,192]{1,0:T(8,128)S(1)} fusion(f32[48,192,64]{2,1,0:T(8,128)} %reshape.87, f32[48,64,192]{2,1,0:T(8,128)S(1)} %reshape.88), kind=kOutput, calls=%fused_computation.3 | convolution fusion | flops 1358954496 | bytes 4866048 | tf_op jit(solution)/shard_map/pnm,pml->nl/dot_general | solution.py:53
  77.3 2.1 %collective-permute-start.6 = (f32[64,192]{1,0:T(8,128)S(1)}, f32[64,192]{1,0:T(8,128)S(1)}, u32[]{:S(2)}, u32[]{:S(2)}) collective-permute-start(f32[64,192]{1,0:T(8,128)S(1)} %get-tuple-element.5), channel_id=1, source_target_pairs={{0,1},{1,2},{2,3},{3,4},{4,5},{5,6},{6,7},{7,8},{8,9},{9,10},{10,1... | collective-permute-start | bytes 147464 | tf_op jit(solution)/shard_map/ppermute | solution.py:16
  79.4 2.4 %collective-permute-start.7 = (f32[64,192]{1,0:T(8,128)S(1)}, f32[64,192]{1,0:T(8,128)S(1)}, u32[]{:S(2)}, u32[]{:S(2)}) collective-permute-start(f32[64,192]{1,0:T(8,128)S(1)} %get-tuple-element.6), channel_id=1, source_target_pairs={{0,15},{1,0},{2,1},{3,2},{4,3},{5,4},{6,5},{7,6},{8,7},{9,8},{10,9... | collective-permute-start | bytes 147464 | tf_op jit(solution)/shard_map/ppermute | solution.py:16
  81.8 2.0 %collective-permute-done.6 = f32[64,192]{1,0:T(8,128)S(1)} collective-permute-done((f32[64,192]{1,0:T(8,128)S(1)}, f32[64,192]{1,0:T(8,128)S(1)}, u32[]{:S(2)}, u32[]{:S(2)}) %collective-permute-start.6) | collective-permute-done | bytes 49184 | tf_op jit(solution)/shard_map/ppermute | solution.py:16
  83.9 0.1 pad_add_fusion
  84.0 5.4 %all-gather = f32[128,320]{1,0:T(8,128)S(1)} all-gather(f32[64,320]{1,0:T(8,128)S(1)} %pad_add_fusion), channel_id=2, replica_groups=mesh['tens'=2,'atom'=16] {'tens'}, dimensions={0}, use_global_device_ids=true | all-gather | bytes 245760 | tf_op jit(solution)/shard_map/all_gather | solution.py:11
  89.4 0.7 reduce_sum.9
  (20 shorter events, 0.4 us)
Async XLA Ops:
  0.0 17.0 %collective-permute-start.4 = (f32[96,256]{1,0:T(8,128)}, f32[96,256]{1,0:T(8,128)S(1)}, u32[]{:S(2)}, u32[]{:S(2)}) collective-permute-start(f32[96,256]{1,0:T(8,128)} %param.5), channel_id=1, source_target_pairs={{0,14},{1,15},{2,0},{3,1},{4,2},{5,3},{6,4},{7,5},{8,6},{9,7},{10,... | collective-permute-start | bytes 294920 | tf_op jit(solution)/shard_map/ppermute | solution.py:16
  6.0 10.9 %collective-permute-start.3 = (f32[96,256]{1,0:T(8,128)}, f32[96,256]{1,0:T(8,128)S(1)}, u32[]{:S(2)}, u32[]{:S(2)}) collective-permute-start(f32[96,256]{1,0:T(8,128)} %param.5), channel_id=1, source_target_pairs={{0,15},{1,0},{2,1},{3,2},{4,3},{5,4},{6,5},{7,6},{8,7},{9,8},{10,9... | collective-permute-start | bytes 294920 | tf_op jit(solution)/shard_map/ppermute | solution.py:16
  6.0 10.0 %collective-permute-start.2 = (f32[96,256]{1,0:T(8,128)}, f32[96,256]{1,0:T(8,128)S(1)}, u32[]{:S(2)}, u32[]{:S(2)}) collective-permute-start(f32[96,256]{1,0:T(8,128)} %param.5), channel_id=1, source_target_pairs={{0,1},{1,2},{2,3},{3,4},{4,5},{5,6},{6,7},{7,8},{8,9},{9,10},{10,1... | collective-permute-start | bytes 294920 | tf_op jit(solution)/shard_map/ppermute | solution.py:16
  6.5 9.5 %collective-permute-start.1 = (f32[96,256]{1,0:T(8,128)}, f32[96,256]{1,0:T(8,128)S(1)}, u32[]{:S(2)}, u32[]{:S(2)}) collective-permute-start(f32[96,256]{1,0:T(8,128)} %param.5), channel_id=1, source_target_pairs={{0,2},{1,3},{2,4},{3,5},{4,6},{5,7},{6,8},{7,9},{8,10},{9,11},{10,... | collective-permute-start | bytes 294920 | tf_op jit(solution)/shard_map/ppermute | solution.py:16
  7.2 6.1 %collective-permute-start = (f32[96,256]{1,0:T(8,128)}, f32[96,256]{1,0:T(8,128)S(1)}, u32[]{:S(2)}, u32[]{:S(2)}) collective-permute-start(f32[96,256]{1,0:T(8,128)} %param.5), channel_id=1, source_target_pairs={{0,3},{1,4},{2,5},{3,6},{4,7},{5,8},{6,9},{7,10},{8,11},{9,12},{10... | collective-permute-start | bytes 294920 | tf_op jit(solution)/shard_map/ppermute | solution.py:16
  13.3 5.8 %collective-permute-start.5 = (f32[96,256]{1,0:T(8,128)}, f32[96,256]{1,0:T(8,128)S(1)}, u32[]{:S(2)}, u32[]{:S(2)}) collective-permute-start(f32[96,256]{1,0:T(8,128)} %param.5), channel_id=1, source_target_pairs={{0,13},{1,14},{2,15},{3,0},{4,1},{5,2},{6,3},{7,4},{8,5},{9,6},{10... | collective-permute-start | bytes 294920 | tf_op jit(solution)/shard_map/ppermute | solution.py:16
  29.1 31.8 %all-to-all-start = ((f32[2,48,6144]{2,1,0:T(8,128)}), f32[2,48,6144]{2,1,0:T(8,128)}, u32[]{:S(2)}, u32[]{:S(2)}) async-start(f32[2,48,6144]{2,1,0:T(8,128)} %fusion), calls=%async_computation | async-start | bytes 4718592 | tf_op jit(solution)/shard_map/all_to_all | solution.py:51
  77.3 6.5 %collective-permute-start.6 = (f32[64,192]{1,0:T(8,128)S(1)}, f32[64,192]{1,0:T(8,128)S(1)}, u32[]{:S(2)}, u32[]{:S(2)}) collective-permute-start(f32[64,192]{1,0:T(8,128)S(1)} %get-tuple-element.5), channel_id=1, source_target_pairs={{0,1},{1,2},{2,3},{3,4},{4,5},{5,6},{6,7},{7,8},{8,9},{9,10},{10,1... | collective-permute-start | bytes 147464 | tf_op jit(solution)/shard_map/ppermute | solution.py:16
  79.4 4.4 %collective-permute-start.7 = (f32[64,192]{1,0:T(8,128)S(1)}, f32[64,192]{1,0:T(8,128)S(1)}, u32[]{:S(2)}, u32[]{:S(2)}) collective-permute-start(f32[64,192]{1,0:T(8,128)S(1)} %get-tuple-element.6), channel_id=1, source_target_pairs={{0,15},{1,0},{2,1},{3,2},{4,3},{5,4},{6,5},{7,6},{8,7},{9,8},{10,9... | collective-permute-start | bytes 147464 | tf_op jit(solution)/shard_map/ppermute | solution.py:16
